TPU v7x, 128 devices: a whole 4x4x4 slice. The times are simulated.
128 devices in a mesh: box: 32 (over y, z, core), tx: 4 (over x).
Axes of the slice: x: 4, y: 4, z: 4, core: 2. Of those that a mesh axis runs over, the one named last changes fastest.
Arguments:
- bank: bfloat16 [512, 1024, 1024], P('box', 'tx'), may hold values from -6 to 6
- pick: int32 [64], replicated, may hold values from 0 to 1023, as said below
- slot_box: int32 [512], replicated, may hold values from 0 to 511, each once
- leaf_factor: bfloat16 [512, 512, 128], P('box'), may hold values from -0.1875 to 0.1875
- self_factor: bfloat16 [9, 512, 64, 128], P(None, 'box'), may hold values from -0.375 to 0.375
- cross_factor: bfloat16 [9, 512, 64, 128], P(None, 'box'), may hold values from -0.375 to 0.375
- target_factor: bfloat16 [512, 64, 4096], P('box'), may hold values from -0.5 to 0.5
Outputs:
- field: bfloat16 [512, 64, 4096], P('box', 'tx')
Inputs may be any that keep to these rules, and one draw needn't show every extreme that they name: `pick`: distinct stored transmitters. `slot_box`: each box once.
All inputs are finite; a program needn't handle non-finite values.
Results may differ from a plain program's by a relative error of at most 0.023.
Values may be sent and summed in bfloat16 or wider, within the bound.
A program may use at most 128 MiB of HBM per device.

v0:
```python
import jax
import jax.numpy as jnp
from jax import lax
from jax.sharding import PartitionSpec as P


def partner_2(block, axis, bit):
    count = lax.axis_size(axis)
    route = []
    for low in range(count):
        high = low | 1 << bit
        if high != low and high < count:
            route += [(low, high), (high, low)]
    return lax.ppermute(block, axis, route)


def complex_times(values, matrix):
    inner = matrix.shape[-2]
    half = matrix.shape[-1] // 2
    first = jnp.einsum(
        "brn,bnk->brk", values[..., :inner], matrix, preferred_element_type=jnp.float32
    )
    second = jnp.einsum(
        "brn,bnk->brk", values[..., inner:], matrix, preferred_element_type=jnp.float32
    )
    return jnp.concatenate(
        [first[..., :half] - second[..., half:], first[..., half:] + second[..., :half]], axis=-1
    )


def per_device(bank, pick, slot_box, leaf_factor, self_factor, cross_factor, target_factor):
    box_dev = bank.shape[0]
    bank_dev = bank.shape[1]
    tx_index = lax.axis_index("tx")
    local_pick = pick - tx_index * bank_dev
    chooser = (local_pick[:, None] == jnp.arange(bank_dev, dtype=jnp.int32)[None, :]).astype(
        jnp.bfloat16
    )
    picked = jnp.einsum("pj,bju->bpu", chooser, bank, preferred_element_type=jnp.float32)
    owned = lax.psum_scatter(picked.astype(jnp.bfloat16), "tx", scatter_dimension=1, tiled=True)
    coefs = complex_times(owned, leaf_factor).astype(jnp.bfloat16)
    box_index = lax.axis_index("box")
    sources = lax.dynamic_slice_in_dim(slot_box, box_index * box_dev, box_dev)
    piece = lax.all_gather(coefs, "box", axis=0, tiled=True)
    count = piece.shape[0]
    taker = (sources[:, None] == jnp.arange(count, dtype=jnp.int32)[None, :]).astype(jnp.bfloat16)
    current = jnp.einsum("sn,nrk->srk", taker, piece, preferred_element_type=jnp.float32).astype(
        jnp.bfloat16
    )
    levels = self_factor.shape[0]
    local_bits = box_dev.bit_length() - 1
    for level in range(levels):
        if level < local_bits:
            span = 1 << level
            shaped = current.reshape(
                box_dev // (2 * span), 2, span, current.shape[1], current.shape[2]
            )
            partner = jnp.flip(shaped, axis=1).reshape(current.shape)
        else:
            partner = partner_2(current, "box", level - local_bits)
        mixed = complex_times(current, self_factor[level]) + complex_times(
            partner, cross_factor[level]
        )
        current = mixed.astype(jnp.bfloat16)
    return complex_times(current, target_factor).astype(jnp.bfloat16)


def solution(mesh):
    in_specs = (
        P("box", "tx", None),
        P(),
        P(),
        P("box", None, None),
        P(None, "box", None, None),
        P(None, "box", None, None),
        P("box", None, None),
    )
    out_specs = P("box", "tx", None)
    return jax.shard_map(
        per_device, mesh=mesh, in_specs=in_specs, out_specs=out_specs, check_vma=False
    )
```

profile of v0, /device:TPU:0, one launch (start us, length us, event | category | flops | bytes accessed | tf_op | source)
XLA Modules:
  0.0 153.6 jit_solution(15288603705547300182)
XLA Ops:
  7.3 6.3 %convert_bitcast_fusion = bf16[16,64,1024]{2,1,0:T(8,128)(2,1)} fusion(bf16[16,256,1024]{2,1,0:T(8,128)(2,1)} %param.7, s32[64]{0:T(128)S(1)} %broadcast_subtract_fusion), kind=kOutput, calls=%fused_computation.7 | convolution fusion | flops 537935872 | bytes 10486016 | tf_op jit(solution)/shard_map/pj,bju->bpu/dot_general | solution.py:39
  13.8 32.2 %reduce-scatter.2.cloned.1.call-done = bf16[16,16,1024]{2,1,0:T(8,128)(2,1)} async-done(((bf16[16,64,1024]{2,1,0:T(8,128)(2,1)}), bf16[16,16,1024]{2,1,0:T(8,128)(2,1)}) %reduce-scatter.2.cloned.1.call-update) | async-done | bytes 524304 | tf_op jit(solution)/shard_map/reduce_scatter | solution.py:40
  46.0 1.4 fusion.7
  49.4 43.1 %all-gather.2.cloned.1.call-done = bf16[512,16,128]{2,1,0:T(8,128)(2,1)} async-done(((bf16[16,16,128]{2,1,0:T(8,128)(2,1)}), bf16[512,16,128]{2,1,0:T(8,128)(2,1)}) %all-gather.2.cloned.1.call-update) | async-done | bytes 2097168 | tf_op jit(solution)/shard_map/all_gather | solution.py:44
  92.6 2.0 %fusion.4 = bf16[16,16,128]{2,0,1:T(8,128)(2,1)S(1)} fusion(bf16[512,16,128]{2,1,0:T(8,128)(2,1)} %all-gather.2.cloned.1.call-done, s32[16]{0:T(128)S(1)} %dynamic_slice.3), kind=kOutput, calls=%fused_computation.8 | convolution fusion | flops 33595392 | bytes 2162752 | tf_op jit(solution)/shard_map/sn,nrk->srk/dot_general | solution.py:47
  94.9 1.2 fusion.75
  98.5 1.1 fusion.79
  100.1 1.2 fusion.67
  102.5 1.2 fusion.71
  105.4 1.2 fusion.59
  107.7 1.2 fusion.63
  110.7 1.3 fusion.51
  113.2 1.4 fusion.55
  118.2 1.3 collective-permute-start.1
  120.0 2.5 %collective-permute-done.1 = bf16[16,16,128]{2,1,0:T(8,128)(2,1)S(1)} collective-permute-done((bf16[16,16,128]{2,1,0:T(8,128)(2,1)S(1)}, bf16[16,16,128]{2,1,0:T(8,128)(2,1)S(1)}, u32[]{:S(2)}, u32[]{:S(2)}) %collective-permute-start.1) | collective-permute-done | bytes 65568 | tf_op jit(solution)/shard_map/ppermute | solution.py:14
  123.3 2.4 %collective-permute-start.2 = (bf16[16,16,128]{2,1,0:T(8,128)(2,1)S(1)}, bf16[16,16,128]{2,1,0:T(8,128)(2,1)S(1)}, u32[]{:S(2)}, u32[]{:S(2)}) collective-permute-start(bf16[16,16,128]{2,1,0:T(8,128)(2,1)S(1)} %fusion.129), channel_id=1, source_target_pairs={{0,16},{16,0},{4,20},{20,4},{8,24},{24,8},{12,28},{28,12},{32,48},... | collective-permute-start | bytes 196616 | tf_op jit(solution)/shard_map/ppermute | solution.py:14
  126.2 2.9 %collective-permute-done.2 = bf16[16,16,128]{2,1,0:T(8,128)(2,1)S(1)} collective-permute-done((bf16[16,16,128]{2,1,0:T(8,128)(2,1)S(1)}, bf16[16,16,128]{2,1,0:T(8,128)(2,1)S(1)}, u32[]{:S(2)}, u32[]{:S(2)}) %collective-permute-start.2) | collective-permute-done | bytes 65568 | tf_op jit(solution)/shard_map/ppermute | solution.py:14
  129.9 1.3 collective-permute-start.3
  131.7 2.5 %collective-permute-done.3 = bf16[16,16,128]{2,1,0:T(8,128)(2,1)S(1)} collective-permute-done((bf16[16,16,128]{2,1,0:T(8,128)(2,1)S(1)}, bf16[16,16,128]{2,1,0:T(8,128)(2,1)S(1)}, u32[]{:S(2)}, u32[]{:S(2)}) %collective-permute-start.3) | collective-permute-done | bytes 65568 | tf_op jit(solution)/shard_map/ppermute | solution.py:14
  134.9 2.7 %collective-permute-start.4 = (bf16[16,16,128]{2,1,0:T(8,128)(2,1)S(1)}, bf16[16,16,128]{2,1,0:T(8,128)(2,1)S(1)}, u32[]{:S(2)}, u32[]{:S(2)}) collective-permute-start(bf16[16,16,128]{2,1,0:T(8,128)(2,1)S(1)} %fusion.131), channel_id=1, source_target_pairs={{0,64},{64,0},{4,68},{68,4},{8,72},{72,8},{12,76},{76,12},{16,80},... | collective-permute-start | bytes 196616 | tf_op jit(solution)/shard_map/ppermute | solution.py:14
  138.2 2.8 %collective-permute-done.4 = bf16[16,16,128]{2,1,0:T(8,128)(2,1)S(1)} collective-permute-done((bf16[16,16,128]{2,1,0:T(8,128)(2,1)S(1)}, bf16[16,16,128]{2,1,0:T(8,128)(2,1)S(1)}, u32[]{:S(2)}, u32[]{:S(2)}) %collective-permute-start.4) | collective-permute-done | bytes 65568 | tf_op jit(solution)/shard_map/ppermute | solution.py:14
  141.7 1.3 fusion.133
  143.0 1.2 fusion.135
  145.3 1.5 pad_maximum_fusion
  (88 shorter events, 22.6 us)
Async XLA Ops:
  6.5 39.4 %copy-start = (bf16[16,512,128]{2,1,0:T(8,128)(2,1)S(1)}, bf16[16,512,128]{2,1,0:T(8,128)(2,1)}, u32[]{:S(2)}) copy-start(bf16[16,512,128]{2,1,0:T(8,128)(2,1)} %param.10) | copy-start | bytes 6291460
  6.5 39.4 %reduce-scatter.2.cloned.1.call-start = ((), (), s32[]{:S(2)}) async-start(), calls=%async_computation.1 | async-start | bytes 2621440 | tf_op jit(solution)/shard_map/reduce_scatter | solution.py:40
  13.7 78.9 %all-gather.2.cloned.1.call-start = ((), (), s32[]{:S(2)}) async-start(), calls=%async_computation.2 | async-start | bytes 2162688 | tf_op jit(solution)/shard_map/all_gather | solution.py:44
  46.0 1.4 copy-start.3
  110.7 5.8 %copy-start.1 = (bf16[9,16,64,128]{3,2,1,0:T(8,128)(2,1)S(1)}, bf16[9,16,64,128]{3,2,1,0:T(8,128)(2,1)}, u32[]{:S(2)}) copy-start(bf16[9,16,64,128]{3,2,1,0:T(8,128)(2,1)} %param.11) | copy-start | bytes 7077892
  113.2 4.3 %copy-start.2 = (bf16[9,16,64,128]{3,2,1,0:T(8,128)(2,1)S(1)}, bf16[9,16,64,128]{3,2,1,0:T(8,128)(2,1)}, u32[]{:S(2)}) copy-start(bf16[9,16,64,128]{3,2,1,0:T(8,128)(2,1)} %param.12) | copy-start | bytes 7077892
  116.1 1.3 collective-permute-start
  118.2 4.3 %collective-permute-start.1 = (bf16[16,16,128]{2,1,0:T(8,128)(2,1)S(1)}, bf16[16,16,128]{2,1,0:T(8,128)(2,1)S(1)}, u32[]{:S(2)}, u32[]{:S(2)}) collective-permute-start(bf16[16,16,128]{2,1,0:T(8,128)(2,1)S(1)} %fusion.128), channel_id=1, source_target_pairs={{0,8},{8,0},{4,12},{12,4},{16,24},{24,16},{20,28},{28,20},{32,40},... | collective-permute-start | bytes 196616 | tf_op jit(solution)/shard_map/ppermute | solution.py:14
  119.9 21.8 %slice-start = ((s8[8388608]{0:T(1024)(128)(4,1)}), s8[4194304]{0:T(1024)(128)(4,1)S(1)}, s32[]{:S(2)}) async-start(s8[8388608]{0:T(1024)(128)(4,1)} %bitcast.120), calls=%async_computation.3 | async-start | bytes 8388608
  123.3 5.8 %collective-permute-start.2 = (bf16[16,16,128]{2,1,0:T(8,128)(2,1)S(1)}, bf16[16,16,128]{2,1,0:T(8,128)(2,1)S(1)}, u32[]{:S(2)}, u32[]{:S(2)}) collective-permute-start(bf16[16,16,128]{2,1,0:T(8,128)(2,1)S(1)} %fusion.129), channel_id=1, source_target_pairs={{0,16},{16,0},{4,20},{20,4},{8,24},{24,8},{12,28},{28,12},{32,48},... | collective-permute-start | bytes 196616 | tf_op jit(solution)/shard_map/ppermute | solution.py:14
  129.8 11.9 %slice-start.1 = ((s8[8388608]{0:T(1024)(128)(4,1)}), s8[4194304]{0:T(1024)(128)(4,1)S(1)}, s32[]{:S(2)}) async-start(s8[8388608]{0:T(1024)(128)(4,1)} %bitcast.120), calls=%async_computation.4 | async-start | bytes 8388608
  129.9 4.3 %collective-permute-start.3 = (bf16[16,16,128]{2,1,0:T(8,128)(2,1)S(1)}, bf16[16,16,128]{2,1,0:T(8,128)(2,1)S(1)}, u32[]{:S(2)}, u32[]{:S(2)}) collective-permute-start(bf16[16,16,128]{2,1,0:T(8,128)(2,1)S(1)} %fusion.130), channel_id=1, source_target_pairs={{0,32},{32,0},{4,36},{36,4},{8,40},{40,8},{12,44},{44,12},{16,48},... | collective-permute-start | bytes 196616 | tf_op jit(solution)/shard_map/ppermute | solution.py:14
  134.9 6.0 %collective-permute-start.4 = (bf16[16,16,128]{2,1,0:T(8,128)(2,1)S(1)}, bf16[16,16,128]{2,1,0:T(8,128)(2,1)S(1)}, u32[]{:S(2)}, u32[]{:S(2)}) collective-permute-start(bf16[16,16,128]{2,1,0:T(8,128)(2,1)S(1)} %fusion.131), channel_id=1, source_target_pairs={{0,64},{64,0},{4,68},{68,4},{8,72},{72,8},{12,76},{76,12},{16,80},... | collective-permute-start | bytes 196616 | tf_op jit(solution)/shard_map/ppermute | solution.py:14
Sparse Core Ops, SparseCore 0:
  13.8 32.0 reduce-scatter.1
  48.8 43.7 all-gather.1
where the time goes:
time: 154 us
  waiting for transfers between devices  86.4 us (56%)
  matrix products  35.8 us (23%)
  between operations  13.9 us (9%)
  other arithmetic  8.3 us (5%)
  starting transfers between devices  7.97 us (5%)
    all_gather x1, waiting for transfers between devices, per_device(): piece = lax.all_gather(coefs, 'box', axis=0, tiled=True)  43.1 us
    reduce_scatter x1, waiting for transfers between devices, per_device(): lax.psum_scatter(picked.astype(jnp.bfloat16), 'tx', scatter_dimension=1,...  32.2 us
    dot_general x20, matrix products, complex_times(): jnp.einsum('brn,bnk->brk', values[..., inner:], matrix, preferred_element...  15 us
    dot_general x20, matrix products, complex_times(): jnp.einsum('brn,bnk->brk', values[..., :inner], matrix, preferred_element...  12.5 us
    ppermute x5, waiting for transfers between devices, partner_2(): return lax.ppermute(block, axis, route)  11 us
    ppermute x5, starting transfers between devices, partner_2(): return lax.ppermute(block, axis, route)  7.93 us
    dot_general x1, matrix products, per_device(): jnp.einsum('pj,bju->bpu', chooser, bank, preferred_element_type=jnp.float32)  6.33 us
  transfers between devices with their start and end apart: 7, of which 7 were waited for; matrix products, arithmetic and copies ran while one was open for 2% of the time, Pallas kernels for 0%

commit v1 on v0

--- a/solution.py
+++ b/solution.py
@@ -41,7 +41,12 @@
     coefs = complex_times(owned, leaf_factor).astype(jnp.bfloat16)
     box_index = lax.axis_index("box")
     sources = lax.dynamic_slice_in_dim(slot_box, box_index * box_dev, box_dev)
-    piece = lax.all_gather(coefs, "box", axis=0, tiled=True)
+
+    def create_column(a0):
+        e_next = jnp.concatenate(lax.axis_size("box") * [a0], axis=0)
+        return lax.all_to_all(e_next, "box", 0, 0, tiled=True)
+
+    piece = create_column(coefs)
     count = piece.shape[0]
     taker = (sources[:, None] == jnp.arange(count, dtype=jnp.int32)[None, :]).astype(jnp.bfloat16)
     current = jnp.einsum("sn,nrk->srk", taker, piece, preferred_element_type=jnp.float32).astype(

time: 154 us -> 167 us (1.084)
  local copies, waits for them, and re-layouts: 1.22 us -> 20.9 us
  waiting for transfers between devices: 86.4 us -> 78.2 us
    all_gather x1 -> x0, waiting for transfers between devices: 43.1 us -> none  [per_device(): piece = lax.all_gather(coefs, 'box', axis=0, tiled=True)]
    all_to_all x0 -> x1, waiting for transfers between devices: none -> 28.1 us  [create_column(): return lax.all_to_all(e_next, 'box', 0, 0, tiled=True)]
    unnamed x12 -> x42, local copies, waits for them, and re-layouts: 0.03 us -> 19 us
    all_to_all x0 -> x1, starting transfers between devices: none -> 7.4 us  [create_column(): return lax.all_to_all(e_next, 'box', 0, 0, tiled=True)]
    ppermute x5, waiting for transfers between devices: 11 us -> 17.8 us  [partner_2(): return lax.ppermute(block, axis, route)]
    ppermute x5, starting transfers between devices: 7.93 us -> 1.57 us  [partner_2(): return lax.ppermute(block, axis, route)]
where the time goes in v1:
time: 167 us; the launch traced here: 166 us
  waiting for transfers between devices  78.2 us (47%)
  matrix products  35.8 us (21%)
  local copies, waits for them, and re-layouts  20.9 us (13%)
  between operations  13.9 us (8%)
  starting transfers between devices  8.98 us (5%)
  other arithmetic  8.3 us (5%)
    reduce_scatter x1, waiting for transfers between devices, per_device(): lax.psum_scatter(picked.astype(jnp.bfloat16), 'tx', scatter_dimension=1,...  32.2 us
    all_to_all x1, waiting for transfers between devices, create_column(): return lax.all_to_all(e_next, 'box', 0, 0, tiled=True)  28.1 us
    unnamed x42, local copies, waits for them, and re-layouts  19 us
    ppermute x5, waiting for transfers between devices, partner_2(): return lax.ppermute(block, axis, route)  17.8 us
    dot_general x20, matrix products, complex_times(): jnp.einsum('brn,bnk->brk', values[..., inner:], matrix, preferred_element...  14.8 us
    dot_general x20, matrix products, complex_times(): jnp.einsum('brn,bnk->brk', values[..., :inner], matrix, preferred_element...  12.7 us
    all_to_all x1, starting transfers between devices, create_column(): return lax.all_to_all(e_next, 'box', 0, 0, tiled=True)  7.4 us
    dot_general x1, matrix products, per_device(): jnp.einsum('pj,bju->bpu', chooser, bank, preferred_element_type=jnp.float32)  6.33 us
  transfers between devices with their start and end apart: 7, of which 7 were waited for; matrix products, arithmetic and copies ran while one was open for 2% of the time, Pallas kernels for 0%

profile of v1, /device:TPU:0, one launch (start us, length us, event | category | flops | bytes accessed | tf_op | source)
XLA Modules:
  0.0 166.1 jit_solution(4934034684158686688)
XLA Ops:
  7.3 6.3 %convert_bitcast_fusion = bf16[16,64,1024]{2,1,0:T(8,128)(2,1)} fusion(bf16[16,256,1024]{2,1,0:T(8,128)(2,1)} %param.7, s32[64]{0:T(128)S(1)} %broadcast_subtract_fusion), kind=kOutput, calls=%fused_computation.7 | convolution fusion | flops 537935872 | bytes 10486016 | tf_op jit(solution)/shard_map/pj,bju->bpu/dot_general | solution.py:39
  13.7 32.2 %reduce-scatter.2.cloned.1.call-done = bf16[16,16,1024]{2,1,0:T(8,128)(2,1)} async-done(((bf16[16,64,1024]{2,1,0:T(8,128)(2,1)}), bf16[16,16,1024]{2,1,0:T(8,128)(2,1)}) %reduce-scatter.2.cloned.1.call-update) | async-done | bytes 524304 | tf_op jit(solution)/shard_map/reduce_scatter | solution.py:40
  46.0 1.4 fusion.7
  68.3 7.4 %all-to-all-start = ((bf16[512,16,128]{2,1,0:T(8,128)(2,1)}), bf16[512,16,128]{2,1,0:T(8,128)(2,1)}, u32[]{:S(2)}, u32[]{:S(2)}) async-start(bf16[512,16,128]{2,1,0:T(8,128)(2,1)} %constant_dynamic-update-slice_fusion), calls=%async_computation.1 | async-start | bytes 4194304 | tf_op jit(solution)/shard_map/all_to_all | solution.py:47
  76.5 28.1 %all-to-all-done = bf16[512,16,128]{2,1,0:T(8,128)(2,1)} async-done(((bf16[512,16,128]{2,1,0:T(8,128)(2,1)}), bf16[512,16,128]{2,1,0:T(8,128)(2,1)}, u32[]{:S(2)}, u32[]{:S(2)}) %all-to-all-start) | async-done | bytes 2097184 | tf_op jit(solution)/shard_map/all_to_all | solution.py:47
  104.6 2.0 %fusion.4 = bf16[16,16,128]{2,0,1:T(8,128)(2,1)S(1)} fusion(bf16[512,16,128]{2,1,0:T(8,128)(2,1)} %all-to-all-done, s32[16]{0:T(128)S(1)} %dynamic_slice.3), kind=kOutput, calls=%fused_computation.8 | convolution fusion | flops 33595392 | bytes 2162752 | tf_op jit(solution)/shard_map/sn,nrk->srk/dot_general | solution.py:52
  106.9 1.2 fusion.75
  108.1 1.1 fusion.77
  110.5 1.1 fusion.79
  112.2 1.2 fusion.67
  114.5 1.2 fusion.71
  115.7 1.1 fusion.73
  117.5 1.2 fusion.59
  119.8 1.2 fusion.63
  122.7 1.3 fusion.51
  125.2 1.2 fusion.55
  126.5 1.3 fusion.57
  130.9 3.7 %collective-permute-done.1 = bf16[16,16,128]{2,1,0:T(8,128)(2,1)S(1)} collective-permute-done((bf16[16,16,128]{2,1,0:T(8,128)(2,1)S(1)}, bf16[16,16,128]{2,1,0:T(8,128)(2,1)S(1)}, u32[]{:S(2)}, u32[]{:S(2)}) %collective-permute-start.1) | collective-permute-done | bytes 65568 | tf_op jit(solution)/shard_map/ppermute | solution.py:14
  136.9 4.3 %collective-permute-done.2 = bf16[16,16,128]{2,1,0:T(8,128)(2,1)S(1)} collective-permute-done((bf16[16,16,128]{2,1,0:T(8,128)(2,1)S(1)}, bf16[16,16,128]{2,1,0:T(8,128)(2,1)S(1)}, u32[]{:S(2)}, u32[]{:S(2)}) %collective-permute-start.2) | collective-permute-done | bytes 65568 | tf_op jit(solution)/shard_map/ppermute | solution.py:14
  142.6 4.1 %collective-permute-done.3 = bf16[16,16,128]{2,1,0:T(8,128)(2,1)S(1)} collective-permute-done((bf16[16,16,128]{2,1,0:T(8,128)(2,1)S(1)}, bf16[16,16,128]{2,1,0:T(8,128)(2,1)S(1)}, u32[]{:S(2)}, u32[]{:S(2)}) %collective-permute-start.3) | collective-permute-done | bytes 65568 | tf_op jit(solution)/shard_map/ppermute | solution.py:14
  148.3 5.1 %collective-permute-done.4 = bf16[16,16,128]{2,1,0:T(8,128)(2,1)S(1)} collective-permute-done((bf16[16,16,128]{2,1,0:T(8,128)(2,1)S(1)}, bf16[16,16,128]{2,1,0:T(8,128)(2,1)S(1)}, u32[]{:S(2)}, u32[]{:S(2)}) %collective-permute-start.4) | collective-permute-done | bytes 65568 | tf_op jit(solution)/shard_map/ppermute | solution.py:14
  154.2 1.3 fusion.133
  155.5 1.2 fusion.135
  157.8 1.5 pad_maximum_fusion
  (118 shorter events, 40.3 us)
Async XLA Ops:
  6.5 39.4 %copy-start = (bf16[16,512,128]{2,1,0:T(8,128)(2,1)S(1)}, bf16[16,512,128]{2,1,0:T(8,128)(2,1)}, u32[]{:S(2)}) copy-start(bf16[16,512,128]{2,1,0:T(8,128)(2,1)} %param.10) | copy-start | bytes 6291460
  6.5 39.4 %reduce-scatter.2.cloned.1.call-start = ((), (), s32[]{:S(2)}) async-start(), calls=%async_computation.2 | async-start | bytes 2621440 | tf_op jit(solution)/shard_map/reduce_scatter | solution.py:40
  46.0 1.4 copy-start.3
  68.3 36.3 %all-to-all-start = ((bf16[512,16,128]{2,1,0:T(8,128)(2,1)}), bf16[512,16,128]{2,1,0:T(8,128)(2,1)}, u32[]{:S(2)}, u32[]{:S(2)}) async-start(bf16[512,16,128]{2,1,0:T(8,128)(2,1)} %constant_dynamic-update-slice_fusion), calls=%async_computation.1 | async-start | bytes 4194304 | tf_op jit(solution)/shard_map/all_to_all | solution.py:47
  122.7 5.5 %copy-start.1 = (bf16[9,16,64,128]{3,2,1,0:T(8,128)(2,1)S(1)}, bf16[9,16,64,128]{3,2,1,0:T(8,128)(2,1)}, u32[]{:S(2)}) copy-start(bf16[9,16,64,128]{3,2,1,0:T(8,128)(2,1)} %param.11) | copy-start | bytes 7077892
  126.4 3.1 %copy-start.2 = (bf16[9,16,64,128]{3,2,1,0:T(8,128)(2,1)S(1)}, bf16[9,16,64,128]{3,2,1,0:T(8,128)(2,1)}, u32[]{:S(2)}) copy-start(bf16[9,16,64,128]{3,2,1,0:T(8,128)(2,1)} %param.12) | copy-start | bytes 7077892
  128.2 1.3 collective-permute-start
  130.2 4.3 %collective-permute-start.1 = (bf16[16,16,128]{2,1,0:T(8,128)(2,1)S(1)}, bf16[16,16,128]{2,1,0:T(8,128)(2,1)S(1)}, u32[]{:S(2)}, u32[]{:S(2)}) collective-permute-start(bf16[16,16,128]{2,1,0:T(8,128)(2,1)S(1)} %fusion.128), channel_id=1, source_target_pairs={{0,8},{8,0},{4,12},{12,4},{16,24},{24,16},{20,28},{28,20},{32,40},... | collective-permute-start | bytes 196616 | tf_op jit(solution)/shard_map/ppermute | solution.py:14
  130.8 23.4 %slice-start = ((s8[8388608]{0:T(1024)(128)(4,1)}), s8[4194304]{0:T(1024)(128)(4,1)S(1)}, s32[]{:S(2)}) async-start(s8[8388608]{0:T(1024)(128)(4,1)} %bitcast.120), calls=%async_computation.3 | async-start | bytes 8388608
  135.3 5.8 %collective-permute-start.2 = (bf16[16,16,128]{2,1,0:T(8,128)(2,1)S(1)}, bf16[16,16,128]{2,1,0:T(8,128)(2,1)S(1)}, u32[]{:S(2)}, u32[]{:S(2)}) collective-permute-start(bf16[16,16,128]{2,1,0:T(8,128)(2,1)S(1)} %fusion.129), channel_id=1, source_target_pairs={{0,16},{16,0},{4,20},{20,4},{8,24},{24,8},{12,28},{28,12},{32,48},... | collective-permute-start | bytes 196616 | tf_op jit(solution)/shard_map/ppermute | solution.py:14
  141.9 12.3 %slice-start.1 = ((s8[8388608]{0:T(1024)(128)(4,1)}), s8[4194304]{0:T(1024)(128)(4,1)S(1)}, s32[]{:S(2)}) async-start(s8[8388608]{0:T(1024)(128)(4,1)} %bitcast.120), calls=%async_computation.4 | async-start | bytes 8388608
  141.9 4.8 %collective-permute-start.3 = (bf16[16,16,128]{2,1,0:T(8,128)(2,1)S(1)}, bf16[16,16,128]{2,1,0:T(8,128)(2,1)S(1)}, u32[]{:S(2)}, u32[]{:S(2)}) collective-permute-start(bf16[16,16,128]{2,1,0:T(8,128)(2,1)S(1)} %fusion.130), channel_id=1, source_target_pairs={{0,32},{32,0},{4,36},{36,4},{8,40},{40,8},{12,44},{44,12},{16,48},... | collective-permute-start | bytes 196616 | tf_op jit(solution)/shard_map/ppermute | solution.py:14
  147.4 6.0 %collective-permute-start.4 = (bf16[16,16,128]{2,1,0:T(8,128)(2,1)S(1)}, bf16[16,16,128]{2,1,0:T(8,128)(2,1)S(1)}, u32[]{:S(2)}, u32[]{:S(2)}) collective-permute-start(bf16[16,16,128]{2,1,0:T(8,128)(2,1)S(1)} %fusion.131), channel_id=1, source_target_pairs={{0,64},{64,0},{4,68},{68,4},{8,72},{72,8},{12,76},{76,12},{16,80},... | collective-permute-start | bytes 196616 | tf_op jit(solution)/shard_map/ppermute | solution.py:14
Sparse Core Ops, SparseCore 0:
  13.8 32.0 reduce-scatter.1
